TPU v7x, 32 devices: a whole 2x2x4 slice. The times are simulated.
32 devices in a mesh: stream: 8 (over z, x), cross: 4 (over y, core).
Axes of the slice: x: 2, y: 2, z: 4, core: 2. Of those that a mesh axis runs over, the one named last changes fastest.
Arguments:
- rhs: float32 [128, 320, 128], P(('stream', 'cross')), may hold values from -240 to 240
- damping: float32 [128, 320], P(('stream', 'cross')), may hold values from 3 to 6
- omega: float32 [1], replicated, may hold values from 1 to 3
- jac_diag: bfloat16 [128, 320, 320], P(('stream', 'cross')), may hold values from -0.15625 to 0.15625
- jac_face: bfloat16 [128, 320, 480], P(('stream', 'cross')), may hold values from -0.125 to 0.125
- face_list: int32 [128, 6], P(('stream', 'cross')), may hold values from 0 to 36, as said below
- stream_sends: int32 [32, 2, 4], P(('stream', 'cross')), may hold values from 0 to 19, as said below
- cross_sends: int32 [32, 2, 2], P(('stream', 'cross')), may hold values from 0 to 23, as said below
Outputs:
- solution: float32 [128, 320, 128], P(('stream', 'cross'))
- residual: float32 [128, 320, 128], P(('stream', 'cross'))
Inputs may be any that keep to these rules, and one draw needn't show every extreme that they name: `face_list`: within each partition, each face of an element points to the opposite face of its neighbour: to a slot 6 e + f of an own element, to a received trace in the layout of the table, or to the zero last slot on radial boundaries. Every received slot is read by exactly one face. `stream_sends`: each row lists distinct own trace slots 6 e + f of streamwise faces, in the order in which the neighbour's table receives them. `cross_sends`: each row lists distinct own trace slots 6 e + f of azimuthal faces, in the order in which the neighbour's table receives them; the cross partitions close into a loop.
All inputs are finite; a program needn't handle non-finite values.
Results may differ from a plain program's by a relative error of at most 0.003.
The roundings to bfloat16 on the way count: a program that leaves them out, or rounds other values in their place, can miss the bound.
Values may be sent and summed in bfloat16 or wider, within the bound.
No kernel may reach another device: no remote copies, remote signals or barrier semaphores. Data moves between devices by JAX's collectives and lax.ppermute only.
A program may use at most 128 MiB of HBM per device.

v0:
```python
import jax
import jax.numpy as jnp
import numpy as np
from jax import lax
from jax.sharding import PartitionSpec as P

NP = 4
NVAR = 5
ITERS = 3


def passed_along(value, axis, steps):
    count = lax.axis_size(axis)
    first, last = (max(0, -steps), min(count, count - steps))
    return lax.ppermute(value, axis, [(source, source + steps) for source in range(first, last)])


def shifted(block, axis, distance):
    devices = range(lax.axis_size(axis))
    route = [((i - distance) % len(devices), i) for i in devices]
    return lax.ppermute(block, axis, route)


def inner(left, right):
    width = left.shape[-1] // 2
    return lax.dot_general(
        left.reshape(-1, width),
        right.reshape(-1, width),
        (((0,), (0,)), ((), ())),
        precision=lax.Precision.HIGHEST,
        preferred_element_type=jnp.float32,
    )


def combine(field, matrix):
    width = matrix.shape[0]
    flat = field.reshape(-1, width)
    return jnp.dot(
        flat, matrix, precision=lax.Precision.HIGHEST, preferred_element_type=jnp.float32
    ).reshape(field.shape)


def small_dot(left, right):
    return jnp.dot(left, right, precision=lax.Precision.HIGHEST, preferred_element_type=jnp.float32)


def orthonormal(field, gram):
    lower = jnp.linalg.cholesky(gram)
    inverse = lax.linalg.triangular_solve(
        lower, jnp.eye(gram.shape[0], dtype=gram.dtype), left_side=True, lower=True
    )
    return (combine(field, inverse.T), lower.T)


def face_rows():
    grid = np.arange(NVAR * NP * NP * NP).reshape(NVAR, NP, NP, NP)
    faces = [
        grid[:, 0],
        grid[:, NP - 1],
        grid[:, :, 0],
        grid[:, :, NP - 1],
        grid[:, :, :, 0],
        grid[:, :, :, NP - 1],
    ]
    return np.concatenate([item.reshape(-1) for item in faces]).astype(np.int32)


def face_traces(rounded):
    count = rounded.shape[0]
    columns = rounded.shape[-1]
    picked = jnp.take(rounded, jnp.asarray(face_rows()), axis=1)
    return picked.reshape(count * 6, NVAR * NP * NP, columns)


def rotate(field):
    half = field.shape[-1] // 2
    return jnp.concatenate([-field[..., half:], field[..., :half]], axis=-1)


def start_block(rhs):
    width = rhs.shape[-1] // 2
    real_part = rhs[..., :width]
    imag_part = rhs[..., width:]
    return jnp.concatenate([real_part, -imag_part, imag_part, real_part], axis=-1)


def least_squares(hessenberg, first_upper):
    height = hessenberg.shape[0]
    width = first_upper.shape[0]
    target = jnp.zeros((height, width), first_upper.dtype).at[:width].set(first_upper)
    normal = small_dot(hessenberg.T, hessenberg)
    right = small_dot(hessenberg.T, target)
    lower = jnp.linalg.cholesky(normal)
    middle = lax.linalg.triangular_solve(lower, right, left_side=True, lower=True)
    coeffs = lax.linalg.triangular_solve(
        lower, middle, left_side=True, lower=True, transpose_a=True
    )
    leftover = target - small_dot(hessenberg, coeffs)
    return (coeffs, leftover)


def lengths_sum(field):
    return lax.psum(inner(field, field), ("stream", "cross"))


def body(rhs, damping, omega, jac_diag, jac_face, face_list, stream_sends, cross_sends):
    count = rhs.shape[0]
    blocksize = rhs.shape[-1]
    columns = 2 * blocksize
    listing = face_list.reshape(-1)
    block = start_block(rhs)
    first, first_upper = orthonormal(block, lengths_sum(block))
    basis = [first]
    hessenberg = jnp.zeros(((ITERS + 1) * blocksize, ITERS * blocksize), jnp.float32)
    for step in range(ITERS):
        field = basis[step]
        rounded = field.astype(jnp.bfloat16)
        traces = face_traces(rounded)
        stream_pack = traces[stream_sends[0]]
        cross_pack = traces[cross_sends[0]]
        from_prev = passed_along(stream_pack[0], "stream", 1)
        from_next = passed_along(stream_pack[1], "stream", -1)
        cross_prev = shifted(cross_pack[0], "cross", 1)
        cross_next = shifted(cross_pack[1], "cross", -1)
        interior = jnp.einsum("eij,ejc->eic", jac_diag, rounded, preferred_element_type=jnp.float32)
        zero_slot = jnp.zeros((1,) + traces.shape[1:], traces.dtype)
        table = jnp.concatenate(
            [traces, from_prev, from_next, cross_prev, cross_next, zero_slot], axis=0
        )
        gathered = table[listing].reshape(count, -1, columns)
        coupled = jnp.einsum("eik,ekc->eic", jac_face, gathered, preferred_element_type=jnp.float32)
        image = interior + coupled + damping[:, :, None] * field + omega[0] * rotate(field)
        local = jnp.stack([inner(vector, image) for vector in basis])
        coeffs = lax.psum(local, ("stream", "cross"))
        for number, vector in enumerate(basis):
            image = image - combine(vector, coeffs[number])
        gram = lengths_sum(image)
        fresh, upper = orthonormal(image, gram)
        for number in range(step + 1):
            hessenberg = hessenberg.at[
                number * blocksize : (number + 1) * blocksize,
                step * blocksize : (step + 1) * blocksize,
            ].set(coeffs[number])
        hessenberg = hessenberg.at[
            (step + 1) * blocksize : (step + 2) * blocksize,
            step * blocksize : (step + 1) * blocksize,
        ].set(upper)
        basis.append(fresh)
    weights, leftover = least_squares(hessenberg, first_upper)
    result = combine(basis[0], weights[:blocksize])
    for step in range(1, ITERS):
        result = result + combine(basis[step], weights[step * blocksize : (step + 1) * blocksize])
    remain = combine(basis[0], leftover[:blocksize])
    for step in range(1, ITERS + 1):
        remain = remain + combine(basis[step], leftover[step * blocksize : (step + 1) * blocksize])
    width = blocksize // 2
    solution = jnp.concatenate(
        [result[..., :width], result[..., blocksize : blocksize + width]], axis=-1
    )
    residual = jnp.concatenate(
        [remain[..., :width], remain[..., blocksize : blocksize + width]], axis=-1
    )
    return (solution, residual)


def solution(mesh):
    in_specs = (
        P(("stream", "cross"), None, None),
        P(("stream", "cross"), None),
        P(),
        P(("stream", "cross"), None, None),
        P(("stream", "cross"), None, None),
        P(("stream", "cross"), None),
        P(("stream", "cross"), None, None),
        P(("stream", "cross"), None, None),
    )
    out_specs = (P(("stream", "cross"), None, None), P(("stream", "cross"), None, None))
    return jax.shard_map(body, mesh=mesh, in_specs=in_specs, out_specs=out_specs, check_vma=False)
```

profile of v0, /device:TPU:1, one launch (start us, length us, event | category | flops | bytes accessed | tf_op | source)
XLA Modules:
  0.0 1384.4 jit_solution(1808762299347239370)
XLA Ops:
  17.7 120.6 %all-reduce.11.cloned.1.call-done = f32[128,128]{0,1:T(8,128)} async-done(((f32[128,128]{0,1:T(8,128)}), f32[128,128]{0,1:T(8,128)}) %all-reduce.11.cloned.1.call-update) | async-done | bytes 65552 | tf_op jit(solution)/shard_map/psum | solution.py:103
  140.1 11.7 cholesky.237
  153.2 9.8 custom-call.35
  171.4 3.8 gather_fusion.9
  181.7 3.7 collective-permute-start
  201.9 3.8 fusion.8
  208.1 4.2 fusion.103
  212.9 121.7 %all-reduce.13.cloned.1.call-done = f32[128,128]{1,0:T(8,128)} async-done(((f32[128,128]{1,0:T(8,128)}), f32[128,128]{1,0:T(8,128)}) %all-reduce.13.cloned.1.call-update) | async-done | bytes 65552 | tf_op jit(solution)/shard_map/psum | solution.py:134
  334.7 3.1 fusion.104
  345.7 4.6 fusion.105
  351.1 120.0 %all-reduce.15.cloned.1.call-done = f32[128,128]{0,1:T(8,128)} async-done(((f32[128,128]{0,1:T(8,128)}), f32[128,128]{0,1:T(8,128)}) %all-reduce.15.cloned.1.call-update) | async-done | bytes 65552 | tf_op jit(solution)/shard_map/psum | solution.py:103
  473.5 12.5 cholesky.248
  489.5 11.3 custom-call.36
  501.9 3.6 fusion.106
  511.6 3.8 gather_fusion.10
  522.7 3.1 fusion.114
  527.8 3.7 collective-permute-start.4
  544.7 3.1 gather_fusion.5
  547.8 4.1 fusion.5
  554.3 3.7 convolution_bitcast_fusion.4
  561.0 123.1 %all-reduce.17.cloned.1.call-done = f32[2,128,128]{2,1,0:T(8,128)} async-done(((f32[2,128,128]{2,1,0:T(8,128)}), f32[2,128,128]{2,1,0:T(8,128)}) %all-reduce.17.cloned.1.call-update) | async-done | bytes 131088 | tf_op jit(solution)/shard_map/psum | solution.py:134
  689.8 3.6 fusion.69
  696.0 3.5 subtract_subtract_fusion.1
  701.8 4.6 fusion.107
  713.3 114.4 %all-reduce.19.cloned.1.call-done = f32[128,128]{0,1:T(8,128)} async-done(((f32[128,128]{0,1:T(8,128)}), f32[128,128]{0,1:T(8,128)}) %all-reduce.19.cloned.1.call-update) | async-done | bytes 65552 | tf_op jit(solution)/shard_map/psum | solution.py:103
  830.2 12.5 cholesky.259
  846.1 11.3 custom-call.37
  858.5 3.6 fusion.108
  868.3 3.7 gather_fusion.11
  884.4 3.7 collective-permute-start.8
  901.3 3.1 gather_fusion.8
  904.4 4.1 fusion.2
  910.9 3.7 convolution_bitcast_fusion.2
  920.3 123.1 %all-reduce.21.cloned.1.call-done = f32[3,128,128]{2,1,0:T(8,128)} async-done(((f32[3,128,128]{2,1,0:T(8,128)}), f32[3,128,128]{2,1,0:T(8,128)}) %all-reduce.21.cloned.1.call-update) | async-done | bytes 196624 | tf_op jit(solution)/shard_map/psum | solution.py:134
  1049.1 3.6 fusion.72
  1055.3 3.6 fusion.74
  1061.6 4.0 subtract_subtract_fusion
  1068.0 4.6 fusion.109
  1079.8 115.8 %all-reduce.23.cloned.1.call-done = f32[128,128]{0,1:T(8,128)} async-done(((f32[128,128]{0,1:T(8,128)}), f32[128,128]{0,1:T(8,128)}) %all-reduce.23.cloned.1.call-update) | async-done | bytes 65552 | tf_op jit(solution)/shard_map/psum | solution.py:103
  1198.1 12.5 cholesky.270
  1220.7 12.5 cholesky.87
  1234.7 10.6 custom-call.29
  1249.5 12.3 cholesky.160
  1264.5 10.4 custom-call.30
  1278.6 12.5 cholesky.179
  1296.1 10.2 while.11
  1306.2 31.1 %custom-call.31 = f32[3,128,128]{1,2,0:T(8,128)} custom-call(f32[3,128,128]{2,1,0:T(8,128)} %get-tuple-element.132), custom_call_target="InvertDiagBlocksLowerTriangular" | custom-call | tf_op jit(solution)/shard_map/triangular_solve | solution.py:95
  1347.2 10.6 custom-call.38
  (311 shorter events, 248.4 us)
Async XLA Ops:
  7.2 194.7 %copy-start = (bf16[4,320,480]{2,1,0:T(8,128)(2,1)S(1)}, bf16[4,320,480]{2,1,0:T(8,128)(2,1)}, u32[]{:S(2)}) copy-start(bf16[4,320,480]{2,1,0:T(8,128)(2,1)} %param.40) | copy-start | bytes 3686404
  7.2 131.1 %all-reduce.11.cloned.1.call-start = ((), (), s32[]{:S(2)}) async-start(), calls=%async_computation | async-start | bytes 131072 | tf_op jit(solution)/shard_map/psum | solution.py:103
  11.9 2.9 copy-start.11
  11.9 3.5 copy-start.42
  11.9 3.5 copy-start.44
  11.9 3.6 copy-start.45
  11.9 3.7 copy-start.43
  11.9 4.4 copy-start.47
  14.8 319.8 %all-reduce.13.cloned.1.call-start = ((), (), s32[]{:S(2)}) async-start(), calls=%async_computation.1 | async-start | bytes 131072 | tf_op jit(solution)/shard_map/psum | solution.py:134
  15.7 183.1 %copy-start.41 = (s32[1024]{0:T(1024)}, s32[1024]{0:T(1024)S(1)}, u32[]{:S(2)}) copy-start(s32[1024]{0:T(1024)S(1)} %pad_clamp_fusion) | copy-start | bytes 12292
  17.0 160.4 %copy-start.40 = (s32[1024]{0:T(1024)}, s32[1024]{0:T(1024)S(1)}, u32[]{:S(2)}) copy-start(s32[1024]{0:T(1024)S(1)} %get-tuple-element.192) | copy-start | bytes 12292
  153.1 1184.2 %copy-start.31 = (f32[128,128]{0,1:T(8,128)}, f32[128,128]{0,1:T(8,128)S(1)}, u32[]{:S(2)}) copy-start(f32[128,128]{0,1:T(8,128)S(1)} %get-tuple-element.179) | copy-start | bytes 196612
  181.7 12.0 collective-permute-start
  185.4 9.9 collective-permute-start.1
  193.0 3.9 collective-permute-start.2
  193.2 4.4 collective-permute-start.3
  195.3 6.6 copy-start.22
  195.3 6.6 copy-start.39
  212.3 258.8 %all-reduce.15.cloned.1.call-start = ((), (), s32[]{:S(2)}) async-start(), calls=%async_computation.2 | async-start | bytes 131072 | tf_op jit(solution)/shard_map/psum | solution.py:103
  345.7 5.4 copy-start.38
  350.3 333.8 %all-reduce.17.cloned.1.call-start = ((), (), s32[]{:S(2)}) async-start(), calls=%async_computation.3 | async-start | bytes 262144 | tf_op jit(solution)/shard_map/psum | solution.py:134
  522.7 3.1 copy-start.9
  525.9 6.9 copy-start.29
  525.9 7.6 copy-start.15
  527.8 8.4 collective-permute-start.4
  531.5 8.0 collective-permute-start.5
  534.5 6.5 collective-permute-start.6
  534.7 7.9 collective-permute-start.7
  554.3 3.7 copy-start.1
  554.3 3.7 copy-start.13
  558.0 3.0 copy-start.37
  560.9 266.8 %all-reduce.19.cloned.1.call-start = ((), (), s32[]{:S(2)}) async-start(), calls=%async_computation.4 | async-start | bytes 131072 | tf_op jit(solution)/shard_map/psum | solution.py:103
  706.5 336.8 %all-reduce.21.cloned.1.call-start = ((), (), s32[]{:S(2)}) async-start(), calls=%async_computation.5 | async-start | bytes 393216 | tf_op jit(solution)/shard_map/psum | solution.py:134
  879.4 3.1 copy-start.8
  882.5 6.9 copy-start.28
  882.5 7.6 copy-start.14
  884.4 8.2 collective-permute-start.8
  888.1 7.9 collective-permute-start.9
  891.1 6.5 collective-permute-start.10
  891.3 7.9 collective-permute-start.11
  910.9 3.7 copy-start.2
  910.9 3.7 copy-start.12
  916.9 3.4 copy-start.36
  919.8 275.8 %all-reduce.23.cloned.1.call-start = ((), (), s32[]{:S(2)}) async-start(), calls=%async_computation.6 | async-start | bytes 131072 | tf_op jit(solution)/shard_map/psum | solution.py:103
  1247.2 48.9 %copy-start.46 = (s32[3]{0:T(128)S(1)}, s32[3]{0:T(128)}, u32[]{:S(2)}) copy-start(s32[3]{0:T(128)} %iota_multiply_fusion) | copy-start | bytes 40
  1337.3 3.7 copy-start.27
  1337.3 4.0 copy-start.20
  1338.8 4.4 copy-start.32
  (19 other events, 29.2 us)
Sparse Core Ops, SparseCore 0:
  14.9 123.3 all-reduce.10
  212.4 122.2 all-reduce.12
  350.5 120.5 all-reduce.14
  561.0 123.0 all-reduce.16
  706.6 121.0 all-reduce.18
  919.9 123.3 all-reduce.20
  1072.8 122.8 all-reduce.22
where the time goes:
time: 1390 us; the launch traced here: 1380 us
  waiting for transfers between devices  842 us (61%)
  other arithmetic  236 us (17%)
  local copies, waits for them, and re-layouts  152 us (11%)
  matrix products  117 us (8%)
  starting transfers between devices  18.9 us (1%)
  between operations  17.7 us (1%)
    psum x4, waiting for transfers between devices, lengths_sum(): return lax.psum(inner(field, field), ('stream', 'cross'))  471 us
    psum x3, waiting for transfers between devices, body(): coeffs = lax.psum(local, ('stream', 'cross'))  368 us
    another operation x11, other arithmetic, least_squares(): lower = jnp.linalg.cholesky(normal)  63.1 us
    another operation x12, other arithmetic, orthonormal(): lower = jnp.linalg.cholesky(gram)  52 us
    another operation x7, other arithmetic, orthonormal(): lax.linalg.triangular_solve(lower, jnp.eye(gram.shape[0], dtype=gram.dtyp...  48.6 us
    dot_general x17, matrix products, combine(): jnp.dot(flat, matrix, precision=lax.Precision.HIGHEST, preferred_element_...  41.9 us
    dot_general x10, matrix products, inner(): lax.dot_general(left.reshape(-1, width), right.reshape(-1, width), (((0,)...  34.9 us
    another operation x3, other arithmetic, least_squares(): lax.linalg.triangular_solve(lower, middle, left_side=True, lower=True, tr...  33.5 us
  transfers between devices with their start and end apart: 19, of which 9 were waited for; matrix products, arithmetic and copies ran while one was open for 3% of the time, Pallas kernels for 0%

commit v1 on v0

--- a/solution.py
+++ b/solution.py
@@ -7,6 +7,10 @@
 NP = 4
 NVAR = 5
 ITERS = 3
+
+
+def expand_the_inputs(frame):
+    return lax.all_gather(frame, ("stream", "cross")).sum(axis=0)
 
 
 def passed_along(value, axis, steps):
@@ -100,7 +104,7 @@
 
 
 def lengths_sum(field):
-    return lax.psum(inner(field, field), ("stream", "cross"))
+    return expand_the_inputs(inner(field, field))
 
 
 def body(rhs, damping, omega, jac_diag, jac_face, face_list, stream_sends, cross_sends):

time: 1390 us -> 1130 us (0.81)
  waiting for transfers between devices: 842 us -> 581 us
    psum x4 -> x0, waiting for transfers between devices: 471 us -> none  [lengths_sum(): return lax.psum(inner(field, field), ('stream', 'cross'))]
    all_gather x0 -> x4, waiting for transfers between devices: none -> 203 us  [expand_the_inputs(): return lax.all_gather(frame, ('stream', 'cross')).sum(axis=0)]
  transfers between devices with their start and end apart: 19 -> 19, of which waited for: 9 -> 9; matrix products, arithmetic and copies ran while one was open for 3% -> 4% of each run, Pallas kernels for 0% -> 0%
where the time goes in v1:
time: 1130 us; the launch traced here: 1120 us
  waiting for transfers between devices  581 us (51%)
  other arithmetic  241 us (21%)
  local copies, waits for them, and re-layouts  145 us (13%)
  matrix products  115 us (10%)
  starting transfers between devices  18.4 us (2%)
  between operations  17.8 us (2%)
    psum x3, waiting for transfers between devices, body(): coeffs = lax.psum(local, ('stream', 'cross'))  372 us
    all_gather x4, waiting for transfers between devices, expand_the_inputs(): return lax.all_gather(frame, ('stream', 'cross')).sum(axis=0)  203 us
    another operation x11, other arithmetic, least_squares(): lower = jnp.linalg.cholesky(normal)  68.5 us
    another operation x12, other arithmetic, orthonormal(): lower = jnp.linalg.cholesky(gram)  51.9 us
    another operation x7, other arithmetic, orthonormal(): lax.linalg.triangular_solve(lower, jnp.eye(gram.shape[0], dtype=gram.dtyp...  44.8 us
    dot_general x17, matrix products, combine(): jnp.dot(flat, matrix, precision=lax.Precision.HIGHEST, preferred_element_...  41.9 us
    dot_general x10, matrix products, inner(): lax.dot_general(left.reshape(-1, width), right.reshape(-1, width), (((0,)...  34.8 us
    another operation x3, other arithmetic, least_squares(): lax.linalg.triangular_solve(lower, middle, left_side=True, lower=True, tr...  33 us
  transfers between devices with their start and end apart: 19, of which 9 were waited for; matrix products, arithmetic and copies ran while one was open for 4% of the time, Pallas kernels for 0%

profile of v1, /device:TPU:1, one launch (start us, length us, event | category | flops | bytes accessed | tf_op | source)
XLA Modules:
  0.0 1118.2 jit_solution(8267456087667890245)
XLA Ops:
  16.4 57.3 %all-gather.9.cloned.1.call-done = f32[4096,128]{1,0:T(8,128)} async-done(((f32[128,128]{1,0:T(8,128)}), f32[4096,128]{1,0:T(8,128)}) %all-gather.9.cloned.1.call-update) | async-done | bytes 2097168 | tf_op jit(solution)/shard_map/all_gather | solution.py:13
  75.5 11.7 %cholesky.237 = f32[128,128]{1,0:T(8,128)S(1)} custom-call(f32[128,128]{1,0:T(8,128)S(1)} %fusion.56), custom_call_target="Cholesky" | custom-call | tf_op jit(solution)/shard_map/jit(cholesky)/cholesky | solution.py:52
  88.5 9.8 custom-call.35
  106.8 3.8 gather_fusion.9
  117.1 3.7 collective-permute-start
  136.9 3.9 fusion.8
  143.1 4.2 fusion.103
  147.4 122.5 %all-reduce.7.cloned.1.call-done = f32[128,128]{1,0:T(8,128)} async-done(((f32[128,128]{1,0:T(8,128)}), f32[128,128]{1,0:T(8,128)}) %all-reduce.7.cloned.1.call-update) | async-done | bytes 65552 | tf_op jit(solution)/shard_map/psum | solution.py:138
  269.9 3.1 fusion.104
  280.9 4.6 fusion.105
  285.8 55.9 %all-gather.11.cloned.1.call-done = f32[4096,128]{1,0:T(8,128)} async-done(((f32[128,128]{1,0:T(8,128)}), f32[4096,128]{1,0:T(8,128)}) %all-gather.11.cloned.1.call-update) | async-done | bytes 2097168 | tf_op jit(solution)/shard_map/all_gather | solution.py:13
  343.5 11.7 %cholesky.248 = f32[128,128]{1,0:T(8,128)S(1)} custom-call(f32[128,128]{1,0:T(8,128)S(1)} %fusion.54), custom_call_target="Cholesky" | custom-call | tf_op jit(solution)/shard_map/jit(cholesky)/cholesky | solution.py:52
  357.1 9.8 custom-call.36
  367.2 3.6 fusion.106
  376.2 3.7 gather_fusion.10
  406.1 3.8 fusion.5
  412.3 3.7 convolution_bitcast_fusion.4
  419.0 124.8 %all-reduce.9.cloned.1.call-done = f32[2,128,128]{2,1,0:T(8,128)} async-done(((f32[2,128,128]{2,1,0:T(8,128)}), f32[2,128,128]{2,1,0:T(8,128)}) %all-reduce.9.cloned.1.call-update) | async-done | bytes 131088 | tf_op jit(solution)/shard_map/psum | solution.py:138
  543.7 3.1 fusion.68
  549.5 3.6 fusion.69
  555.7 3.5 subtract_subtract_fusion.1
  561.6 4.6 fusion.107
  566.4 56.4 %all-gather.13.cloned.1.call-done = f32[4096,128]{1,0:T(8,128)} async-done(((f32[128,128]{1,0:T(8,128)}), f32[4096,128]{1,0:T(8,128)}) %all-gather.13.cloned.1.call-update) | async-done | bytes 2097168 | tf_op jit(solution)/shard_map/all_gather | solution.py:13
  624.6 11.7 %cholesky.259 = f32[128,128]{1,0:T(8,128)S(1)} custom-call(f32[128,128]{1,0:T(8,128)S(1)} %fusion.52), custom_call_target="Cholesky" | custom-call | tf_op jit(solution)/shard_map/jit(cholesky)/cholesky | solution.py:52
  638.2 9.8 custom-call.37
  648.4 3.6 fusion.108
  657.3 3.8 gather_fusion.11
  687.3 3.8 fusion.2
  693.5 3.7 convolution_bitcast_fusion.2
  702.9 124.7 %all-reduce.11.cloned.1.call-done = f32[3,128,128]{2,1,0:T(8,128)} async-done(((f32[3,128,128]{2,1,0:T(8,128)}), f32[3,128,128]{2,1,0:T(8,128)}) %all-reduce.11.cloned.1.call-update) | async-done | bytes 196624 | tf_op jit(solution)/shard_map/psum | solution.py:138
  833.3 3.6 fusion.72
  839.5 3.6 fusion.74
  845.8 4.0 subtract_subtract_fusion
  852.2 4.6 fusion.109
  862.0 3.4 dynamic-slice_select_fusion.1
  865.4 3.7 scatter.36
  872.4 3.4 dynamic-slice_select_fusion
  875.9 3.7 scatter.41
  881.3 33.9 %all-gather.15.cloned.1.call-done = f32[4096,128]{1,0:T(8,128)} async-done(((f32[128,128]{1,0:T(8,128)}), f32[4096,128]{1,0:T(8,128)}) %all-gather.15.cloned.1.call-update) | async-done | bytes 2097168 | tf_op jit(solution)/shard_map/all_gather | solution.py:13
  920.5 13.2 %cholesky.270 = f32[128,128]{1,0:T(8,128)} custom-call(f32[128,128]{1,0:T(8,128)} %fusion.50), custom_call_target="Cholesky" | custom-call | tf_op jit(solution)/shard_map/jit(cholesky)/cholesky | solution.py:52
  947.0 13.2 %cholesky.87 = f32[128,128]{1,0:T(8,128)} custom-call(f32[128,128]{1,0:T(8,128)} %cholesky.279), custom_call_target="Cholesky" | custom-call | tf_op jit(solution)/shard_map/jit(cholesky)/cholesky | solution.py:97
  963.4 11.3 %custom-call.29 = f32[1,128,128]{1,2,0:T(8,128)} custom-call(f32[1,128,128]{2,1,0:T(8,128)} %get-tuple-element.178), custom_call_target="InvertDiagBlocksLowerTriangular" | custom-call | tf_op jit(solution)/shard_map/jit(cholesky)/cholesky | solution.py:97
  979.3 13.2 %cholesky.160 = f32[128,128]{1,0:T(8,128)} custom-call(f32[128,128]{1,0:T(8,128)} %cholesky.283), custom_call_target="Cholesky" | custom-call | tf_op jit(solution)/shard_map/jit(cholesky)/cholesky | solution.py:97
  995.3 11.3 %custom-call.30 = f32[1,128,128]{1,2,0:T(8,128)} custom-call(f32[1,128,128]{2,1,0:T(8,128)} %get-tuple-element.175), custom_call_target="InvertDiagBlocksLowerTriangular" | custom-call | tf_op jit(solution)/shard_map/jit(cholesky)/cholesky | solution.py:97
  1010.2 13.2 %cholesky.179 = f32[128,128]{1,0:T(8,128)} custom-call(f32[128,128]{1,0:T(8,128)} %convolution_subtract_fusion.6), custom_call_target="Cholesky" | custom-call | tf_op jit(solution)/shard_map/jit(cholesky)/cholesky | solution.py:97
  1029.4 10.7 while.11
  1040.1 31.1 %custom-call.31 = f32[3,128,128]{1,2,0:T(8,128)} custom-call(f32[3,128,128]{2,1,0:T(8,128)} %get-tuple-element.132), custom_call_target="InvertDiagBlocksLowerTriangular" | custom-call | tf_op jit(solution)/shard_map/triangular_solve | solution.py:99
  1081.0 10.6 custom-call.38
  (293 shorter events, 245.8 us)
Async XLA Ops:
  7.2 129.7 %copy-start = (bf16[4,320,480]{2,1,0:T(8,128)(2,1)S(1)}, bf16[4,320,480]{2,1,0:T(8,128)(2,1)}, u32[]{:S(2)}) copy-start(bf16[4,320,480]{2,1,0:T(8,128)(2,1)} %param.40) | copy-start | bytes 3686404
  7.2 66.5 %all-gather.9.cloned.1.call-start = ((), (), s32[]{:S(2)}) async-start(), calls=%async_computation.3 | async-start | bytes 2162688 | tf_op jit(solution)/shard_map/all_gather | solution.py:13
  11.9 2.9 copy-start.11
  11.9 3.5 copy-start.34
  11.9 3.6 copy-start.35
  11.9 3.7 copy-start.33
  11.9 4.4 copy-start.32
  14.8 255.1 %all-reduce.7.cloned.1.call-start = ((), (), s32[]{:S(2)}) async-start(), calls=%async_computation | async-start | bytes 131072 | tf_op jit(solution)/shard_map/psum | solution.py:138
  88.5 982.7 %copy-start.27 = (f32[128,128]{0,1:T(8,128)}, f32[128,128]{0,1:T(8,128)S(1)}, u32[]{:S(2)}) copy-start(f32[128,128]{0,1:T(8,128)S(1)} %get-tuple-element.179) | copy-start | bytes 196612
  102.6 1.7 copy-start.9
  117.1 11.6 %collective-permute-start = (bf16[4,80,256]{2,1,0:T(8,128)(2,1)}, bf16[4,80,256]{2,1,0:T(8,128)(2,1)}, u32[]{:S(2)}, u32[]{:S(2)}) collective-permute-start(bf16[4,80,256]{2,1,0:T(8,128)(2,1)} %get-tuple-element.163), channel_id=1, source_target_pairs={{0,4},{4,8},{8,12},{12,16},{16,20},{20,24},{24,28},{1,5},{5,9},{9,... | collective-permute-start | bytes 491528 | tf_op jit(solution)/shard_map/ppermute | solution.py:19
  120.8 9.5 collective-permute-start.1
  123.8 2.9 copy-start.16
  127.8 4.2 collective-permute-start.2
  128.5 4.1 collective-permute-start.3
  130.3 6.6 copy-start.20
  130.3 6.6 copy-start.31
  147.3 194.3 %all-gather.11.cloned.1.call-start = ((), (), s32[]{:S(2)}) async-start(), calls=%async_computation.4 | async-start | bytes 2162688 | tf_op jit(solution)/shard_map/all_gather | solution.py:13
  285.5 258.2 %all-reduce.9.cloned.1.call-start = ((), (), s32[]{:S(2)}) async-start(), calls=%async_computation.1 | async-start | bytes 262144 | tf_op jit(solution)/shard_map/psum | solution.py:138
  386.5 2.9 copy-start.10
  389.4 5.4 copy-start.15
  390.4 6.6 collective-permute-start.4
  393.4 7.1 collective-permute-start.5
  395.8 5.4 collective-permute-start.6
  396.6 5.3 collective-permute-start.7
  412.3 3.7 copy-start.1
  412.3 3.7 copy-start.13
  418.9 203.8 %all-gather.13.cloned.1.call-start = ((), (), s32[]{:S(2)}) async-start(), calls=%async_computation.5 | async-start | bytes 2162688 | tf_op jit(solution)/shard_map/all_gather | solution.py:13
  546.8 2.7 copy-start.30
  566.2 261.4 %all-reduce.11.cloned.1.call-start = ((), (), s32[]{:S(2)}) async-start(), calls=%async_computation.2 | async-start | bytes 393216 | tf_op jit(solution)/shard_map/psum | solution.py:138
  667.6 2.9 copy-start.8
  670.5 5.4 copy-start.14
  671.5 6.4 collective-permute-start.8
  674.6 7.1 collective-permute-start.9
  676.9 5.4 collective-permute-start.10
  677.7 5.2 collective-permute-start.11
  693.5 3.7 copy-start.2
  693.5 3.7 copy-start.12
  697.2 2.2 copy-start.5
  702.4 212.7 %all-gather.15.cloned.1.call-start = ((), (), s32[]{:S(2)}) async-start(), calls=%async_computation.6 | async-start | bytes 2162688 | tf_op jit(solution)/shard_map/all_gather | solution.py:13
  830.6 2.7 copy-start.26
  852.2 5.9 copy-start.36
  1071.2 3.7 copy-start.25
  1071.2 4.0 copy-start.18
  1072.6 4.4 copy-start.28
  1091.9 2.6 copy-start.24
  1101.2 2.4 copy-start.4
  1101.2 2.4 copy-start.17
  (8 other events, 8.8 us)
Sparse Core Ops, SparseCore 0:
  14.9 58.6 all-gather.8
  147.4 122.4 all-reduce.6
  285.6 55.9 all-gather.10
  419.0 124.6 all-reduce.8
  566.3 56.4 all-gather.12
  702.5 124.9 all-reduce.10
  856.9 58.2 all-gather.14
